TPU v7x, 512 devices: a whole 4x4x16 slice. The times are simulated.
512 devices in a mesh: rep: 64 (over x_lo, z, core), fsdp: 8 (over y, x_hi).
Axes of the slice: x: 4 (x_hi: 2, x_lo: 2; x = x_hi * 2 + x_lo), y: 4, z: 16, core: 2. Of those that a mesh axis runs over, the one named last changes fastest.
Arguments:
- hidden_in: bfloat16 [64, 1536, 4096], P('rep', 'fsdp'), may hold values from -6 to 6
- cotangent: bfloat16 [64, 1536, 512], P('rep', 'fsdp'), may hold values from -6 to 6
- weights: float32 [64, 4096, 512], P('rep', 'fsdp'), may hold values from -6 to 6
- moments: bfloat16 [64, 4096, 512], P('rep', 'fsdp'), may hold values from -6 to 6
- norm_gains: bfloat16 [64, 4096], P('rep', 'fsdp'), may hold values from 0.099609375 to 1.8984375
- gain_moments: bfloat16 [64, 4096], P('rep', 'fsdp'), may hold values from -60 to 60
- step_count: int32 [], replicated, may hold values from 0 to 99999
Outputs:
- new_weights: float32 [64, 4096, 512], P('rep', 'fsdp')
- new_moments: bfloat16 [64, 4096, 512], P('rep', 'fsdp')
- new_gains: bfloat16 [64, 4096], P('rep', 'fsdp')
- new_gain_moments: bfloat16 [64, 4096], P('rep', 'fsdp')
All inputs are finite; a program needn't handle non-finite values.
Results may differ from a plain program's by a relative error of at most 0.0061.
Values may be sent and summed in bfloat16 or wider, within the bound.
No kernel may reach another device: no remote copies, remote signals or barrier semaphores. Data moves between devices by JAX's collectives and lax.ppermute only.
A program may use at most 128 MiB of HBM per device.

v0:
```python
from functools import partial

import jax
import jax.numpy as jnp
from jax import lax
from jax.experimental import pallas as pl
from jax.experimental.pallas import tpu as pltpu
from jax.sharding import PartitionSpec as P

D = 4096

norm_eps = 1e-05
momentum_beta = 0.9
learn_weight = 0.25
learn_gain = 0.01
grad_scale = D ** (-0.5)

EXTRA = 8
ROWS = 96
f32, bf16 = jnp.float32, jnp.bfloat16


def from_peer(value, steps):
    count = lax.axis_size("rep")
    return lax.ppermute(value, "rep", [(source, (source - steps) % count) for source in range(count)])


def within_halves(value, steps):
    half = lax.axis_size("rep") // 2
    pairs = [(h * half + i, h * half + (i - steps) % half) for h in range(2) for i in range(half)]
    return lax.ppermute(value, "rep", pairs)


def swap_halves(value, low, high):
    half = lax.axis_size("rep") // 2
    pairs = [(h * half + i, (1 - h) * half + i) for h in range(2) for i in range(low, high)]
    place = lax.rem(lax.axis_index("rep"), half)
    took = (place >= low) & (place < high)
    return lax.ppermute(value, "rep", pairs), took.astype(jnp.int32).reshape(1)


def early_kernel(master_ref, gain_ref, out_ref):
    rows = master_ref.shape[0]
    out_ref[:rows, :] = master_ref[...].astype(bf16)
    out_ref[rows:, :] = jnp.broadcast_to(gain_ref[...], (EXTRA, out_ref.shape[1]))


def pack_kernel(hidden_ref, cotangent_ref, out_ref):
    parts = out_ref.shape[0]
    share = hidden_ref.shape[1] // parts
    hidden = hidden_ref[...].astype(f32)
    inv_rms = lax.rsqrt(jnp.mean(hidden * hidden, axis=-1, keepdims=True) + norm_eps)
    cotangent = cotangent_ref[...]
    for part in range(parts):
        block = hidden_ref[:, part * share : (part + 1) * share].astype(f32)
        out_ref[part, :, :share] = (block * inv_rms).astype(bf16)
        out_ref[part, :, share:] = cotangent


def grad_kernel(got_ref, master_ref, moment_ref, gain_ref, gain_moment_ref, out_ref):
    rows = master_ref.shape[0]
    total = grad_scale * lax.dot_general(
        got_ref[:, :rows],
        got_ref[:, rows:],
        (((0,), (0,)), ((), ())),
        preferred_element_type=f32,
    )
    gain = jnp.transpose(jnp.broadcast_to(gain_ref[...].astype(f32), (128, rows)))[:, :1]
    mom = momentum_beta * moment_ref[...].astype(f32) + gain * total
    out_ref[:rows, :] = mom.astype(bf16)
    add_gain = jnp.sum(master_ref[...].astype(bf16).astype(f32) * total, axis=1, keepdims=True)
    add_gain = jnp.transpose(jnp.broadcast_to(add_gain, (rows, 128)))[:1, :]
    mom_g = momentum_beta * gain_moment_ref[...].astype(f32) + add_gain
    out_ref[rows:, :] = jnp.broadcast_to(mom_g, (EXTRA, rows)).astype(bf16)


def own_step_kernel(master_ref, mom_ref, out_ref):
    rows = master_ref.shape[0]
    out_ref[...] = 0.5 * (master_ref[...] - learn_weight * mom_ref[:rows, :].astype(f32))


def final_kernel(
    took_ref, own_ref, mom_ref, kept_ref, swapped_ref, peer_mom_ref,
    gain_ref, kept_gain_ref, swapped_gain_ref, mom_g_ref, peer_mom_g_ref,
    out_w_ref, out_mom_ref, out_gain_ref, out_gain_mom_ref,
):
    peer_mom = peer_mom_ref[...].astype(f32)
    out_mom_ref[...] = (0.5 * (mom_ref[...].astype(f32) + peer_mom)).astype(bf16)

    def finish(early_ref, early_gain_ref):
        peer_step = early_ref[...].astype(f32) - learn_weight * peer_mom
        out_w_ref[...] = own_ref[...] + 0.5 * peer_step

        @pl.when(pl.program_id(0) == 0)
        def _():
            mom_g = mom_g_ref[...].astype(f32)[:1, :]
            peer_mom_g = peer_mom_g_ref[...].astype(f32)[:1, :]
            peer_gain = early_gain_ref[...].astype(f32)[:1, :]
            own = (gain_ref[...].astype(f32) - learn_gain * mom_g).astype(bf16).astype(f32)
            peer = (peer_gain - learn_gain * peer_mom_g).astype(bf16).astype(f32)
            out_gain_ref[...] = (0.5 * (own + peer)).astype(bf16)
            out_gain_mom_ref[...] = (0.5 * (mom_g + peer_mom_g)).astype(bf16)

    pl.when(took_ref[0] == 0)(partial(finish, kept_ref, kept_gain_ref))
    pl.when(took_ref[0] != 0)(partial(finish, swapped_ref, swapped_gain_ref))


VMEM = pl.BlockSpec(memory_space=pltpu.VMEM)


def whole(distance, hidden_in, cotangent, weights, moments, norm_gains, gain_moments, step_count):
    inputs, upstream, master, moment = hidden_in[0], cotangent[0], weights[0], moments[0]
    tokens, width = inputs.shape
    rows, kv = master.shape
    parts = lax.axis_size("fsdp")
    far = distance * 2 == lax.axis_size("rep")
    far_along = 8 <= distance and not far
    early = pl.pallas_call(
        early_kernel,
        out_shape=jax.ShapeDtypeStruct((rows + EXTRA, kv), bf16),
        name="early",
    )(master, norm_gains)
    half = lax.axis_size("rep") // 2
    peer_early = from_peer(early, distance) if far else within_halves(early, distance)

    def own_step(master, mom):
        return pl.pallas_call(
            own_step_kernel,
            out_shape=jax.ShapeDtypeStruct((rows, kv), f32),
            name="own",
        )(master, mom)

    def between(first, master, mom, peer_early):
        if first:
            peer_early, master = lax.optimization_barrier((peer_early, master))
        swapped, took = swap_halves(peer_early, half - distance, half)
        return own_step(master, mom), swapped, took

    def section(block, *operands):
        inputs, upstream, master, moment, norm_gains, gain_moments = operands[:6]
        packed = pl.pallas_call(
            pack_kernel,
            grid=(tokens // block,),
            in_specs=[
                pl.BlockSpec((block, width), lambda i: (i, 0)),
                pl.BlockSpec((block, kv), lambda i: (i, 0)),
            ],
            out_specs=pl.BlockSpec((parts, block, rows + kv), lambda i: (0, i, 0)),
            out_shape=jax.ShapeDtypeStruct((parts, tokens, rows + kv), bf16),
            name="pack",
        )(inputs, upstream)
        got = lax.all_to_all(packed, "fsdp", split_axis=0, concat_axis=0, tiled=True)
        got = got.reshape(parts * tokens, rows + kv)
        early = operands[6:]
        if early:
            got, *early = lax.optimization_barrier((got, *early))
        got = pltpu.with_memory_space_constraint(got, pltpu.VMEM)
        mom = pl.pallas_call(
            grad_kernel,
            in_specs=[VMEM] * 5,
            out_specs=VMEM,
            out_shape=jax.ShapeDtypeStruct((rows + EXTRA, kv), bf16),
            name="grad",
        )(got, master, moment, norm_gains, gain_moments)
        return (mom, *early)

    operands = (inputs, upstream, master, moment, norm_gains, gain_moments)
    if far_along:
        (mom,) = section(ROWS, *operands)
        peer_mom = from_peer(mom, distance)
        sure = step_count >= 0
        own, swapped, took = lax.cond(
            sure, partial(between, True), partial(between, False), master, mom, peer_early
        )
        peer_mom, own = lax.optimization_barrier((peer_mom, own))
    elif far:
        (mom,) = section(ROWS, *operands)
        swapped, took = early, jnp.zeros((1,), jnp.int32)
    else:
        mom, peer_early = section(ROWS, *operands, peer_early)
        swapped, took = swap_halves(peer_early, half - distance, half)
        if distance == 2:
            peer_early, took = jnp.where(took != 0, swapped, peer_early), jnp.zeros_like(took)
    if not far_along:
        peer_mom = from_peer(mom, distance)
        own = own_step(master, mom)
    return own, mom, peer_mom, peer_early, swapped, took


def shards(hidden_in, cotangent, weights, moments, norm_gains, gain_moments, step_count):
    hop_total = lax.axis_size("rep").bit_length() - 1
    hop_index = lax.rem(step_count, hop_total)
    branches = [partial(whole, 1 << level) for level in range(hop_total)]
    own, mom, peer_mom, peer_early, swapped, took = lax.switch(
        hop_index, branches, hidden_in, cotangent, weights, moments, norm_gains, gain_moments,
        step_count,
    )
    rows, kv = own.shape
    block = rows // 2
    tile = pl.BlockSpec((block, kv), lambda i: (i, 0))
    row = pl.BlockSpec((1, rows), lambda i: (0, 0))
    last = pl.BlockSpec((EXTRA, kv), lambda i: (rows // EXTRA, 0))
    out_w, out_mom, out_gain, out_gain_mom = pl.pallas_call(
        final_kernel,
        grid=(rows // block,),
        in_specs=[pl.BlockSpec(memory_space=pltpu.SMEM)] + [tile] * 5 + [row] + [last] * 4,
        out_specs=[tile, tile, row, row],
        out_shape=[
            jax.ShapeDtypeStruct((rows, kv), f32),
            jax.ShapeDtypeStruct((rows, kv), bf16),
            jax.ShapeDtypeStruct((1, rows), bf16),
            jax.ShapeDtypeStruct((1, rows), bf16),
        ],
        name="final",
    )(
        took, own, mom, peer_early, swapped, peer_mom,
        norm_gains, peer_early, swapped, mom, peer_mom,
    )
    return (out_w[None], out_mom[None], out_gain, out_gain_mom)


def solution(mesh):
    in_specs = (
        P("rep", "fsdp", None),
        P("rep", "fsdp", None),
        P("rep", "fsdp", None),
        P("rep", "fsdp", None),
        P("rep", "fsdp"),
        P("rep", "fsdp"),
        P(),
    )
    out_specs = (P("rep", "fsdp", None), P("rep", "fsdp", None), P("rep", "fsdp"), P("rep", "fsdp"))
    return jax.shard_map(shards, mesh=mesh, in_specs=in_specs, out_specs=out_specs, check_vma=False)
```

profile of v0, /device:TPU:480, one launch (start us, length us, event | category | flops | bytes accessed | tf_op | source)
XLA Modules:
  0.0 82.3 jit_solution(16811738647024765419)
XLA Ops:
  1.3 78.1 %conditional.3 = (f32[512,512]{1,0:T(8,128)}, bf16[520,512]{1,0:T(8,128)(2,1)}, bf16[520,512]{1,0:T(8,128)(2,1)}, bf16[520,512]{1,0:T(8,128)(2,1)}, bf16[520,512]{1,0:T(8,128)(2,1)}, /*index=5*/s32[1]{0:T(128)}) conditional(s32[]{:T(128)} %clamp.3, (f32[1,512,512]{2,1,0:T(8,128)}, bf16[1,192,4096]{2,1,0:T(8,128)(2,1)}, ...), branch_computations={%region_0.0_spmd, %region_1.2_spmd, %region_2.3_spmd, %region_3.6_... | conditional | flops 266254 | bytes 17432972 | solution.py:194
  1.3 3.1 %pack.7 = bf16[8,192,1024]{2,1,0:T(8,128)(2,1)} custom-call(bf16[192,4096]{1,0:T(8,128)(2,1)} %bitcast.65, bf16[192,512]{1,0:T(8,128)(2,1)} %bitcast.77), custom_call_target="tpu_custom_call" | custom-call | tf_op jit(solution)/shard_map/cond/branch_1_fun/pack/pallas_call | solution.py:141
  4.4 0.0 copy-start.1
  4.4 0.0 copy-start.7
  4.5 7.1 %all-to-all-start.5 = ((bf16[8,192,1024]{2,1,0:T(8,128)(2,1)}), bf16[8,192,1024]{2,1,0:T(8,128)(2,1)S(1)}, u32[]{:S(2)}, u32[]{:S(2)}) async-start(bf16[8,192,1024]{2,1,0:T(8,128)(2,1)} %pack.7), calls=%async_computation.5 | async-start | bytes 6291456 | tf_op jit(solution)/shard_map/cond/branch_1_fun/all_to_all | solution.py:152
  11.5 0.0 copy-done.1
  11.5 2.1 %early.7 = bf16[520,512]{1,0:T(8,128)(2,1)} custom-call(f32[512,512]{1,0:T(8,128)} %bitcast.47, bf16[1,512]{1,0:T(2,128)(2,1)S(1)} %copy-done.1), custom_call_target="tpu_custom_call" | custom-call | tf_op jit(solution)/shard_map/cond/branch_1_fun/early/pallas_call | solution.py:118
  13.6 2.9 %collective-permute-start.16 = (bf16[520,512]{1,0:T(8,128)(2,1)}, bf16[520,512]{1,0:T(8,128)(2,1)}, u32[]{:S(2)}, u32[]{:S(2)}) collective-permute-start(bf16[520,512]{1,0:T(8,128)(2,1)} %early.7), channel_id=1, source_target_pairs={{0,240},{8,248},{16,0},{24,8},{32,16},{40,24},{48,32},{56,40},{64,... | collective-permute-start | bytes 1597448 | tf_op jit(solution)/shard_map/cond/branch_1_fun/ppermute | solution.py:31
  16.5 14.1 %collective-permute-done.16 = bf16[520,512]{1,0:T(8,128)(2,1)} collective-permute-done((bf16[520,512]{1,0:T(8,128)(2,1)}, bf16[520,512]{1,0:T(8,128)(2,1)}, u32[]{:S(2)}, u32[]{:S(2)}) %collective-permute-start.16) | collective-permute-done | bytes 532512 | tf_op jit(solution)/shard_map/cond/branch_1_fun/ppermute | solution.py:31
  30.6 20.7 %all-to-all-done.5 = bf16[8,192,1024]{2,1,0:T(8,128)(2,1)S(1)} async-done(((bf16[8,192,1024]{2,1,0:T(8,128)(2,1)}), bf16[8,192,1024]{2,1,0:T(8,128)(2,1)S(1)}, u32[]{:S(2)}, u32[]{:S(2)}) %all-to-all-start.5) | async-done | bytes 3145760 | tf_op jit(solution)/shard_map/cond/branch_1_fun/all_to_all | solution.py:152
  51.2 2.5 %collective-permute-start.18 = (bf16[520,512]{1,0:T(8,128)(2,1)}, bf16[520,512]{1,0:T(8,128)(2,1)}, u32[]{:S(2)}, u32[]{:S(2)}) collective-permute-start(bf16[520,512]{1,0:T(8,128)(2,1)} %collective-permute-done.16), channel_id=1, source_target_pairs={{240,496},{248,504},{496,240},{504,248},{241,497},{249,505},{497,2... | collective-permute-start | bytes 1597448 | tf_op jit(solution)/shard_map/cond/branch_1_fun/ppermute | solution.py:39
  53.7 0.0 copy-done.7
  53.7 3.5 %grad.7.mom_ref = bf16[520,512]{1,0:T(8,128)(2,1)} custom-call(bf16[1536,1024]{1,0:T(8,128)(2,1)S(1)} %bitcast.38, f32[512,512]{1,0:T(8,128)} %bitcast.48, bf16[512,512]{1,0:T(8,128)(2,1)} %bitcast.71, bf16[1,512]{1,0:T(2,128)(2,1)S(1)} %copy-done.1, bf16[1,512]{1,0:T(2,128)(2,1)S(1)} %copy-done.7), custom_call_target="tpu_custom_call" | custom-call | tf_op jit(solution)/shard_map/cond/branch_1_fun/grad/pallas_call | solution.py:158
  57.2 1.9 %collective-permute-start.17 = (bf16[520,512]{1,0:T(8,128)(2,1)}, bf16[520,512]{1,0:T(8,128)(2,1)}, u32[]{:S(2)}, u32[]{:S(2)}) collective-permute-start(bf16[520,512]{1,0:T(8,128)(2,1)} %grad.7.mom_ref), channel_id=1, source_target_pairs={{0,496},{8,504},{16,0},{24,8},{32,16},{40,24},{48,32},{56,40},{64,... | collective-permute-start | bytes 1597448 | tf_op jit(solution)/shard_map/cond/branch_1_fun/ppermute | solution.py:25
  59.1 2.5 %own.9 = f32[512,512]{1,0:T(8,128)} custom-call(f32[512,512]{1,0:T(8,128)} %bitcast.49, bf16[520,512]{1,0:T(8,128)(2,1)} %grad.7.mom_ref), custom_call_target="tpu_custom_call" | custom-call | tf_op jit(solution)/shard_map/cond/branch_1_fun/own/pallas_call | solution.py:127
  61.6 15.8 %collective-permute-done.18 = bf16[520,512]{1,0:T(8,128)(2,1)} collective-permute-done((bf16[520,512]{1,0:T(8,128)(2,1)}, bf16[520,512]{1,0:T(8,128)(2,1)}, u32[]{:S(2)}, u32[]{:S(2)}) %collective-permute-start.18) | collective-permute-done | bytes 532512 | tf_op jit(solution)/shard_map/cond/branch_1_fun/ppermute | solution.py:39
  77.4 1.9 %broadcast_select_fusion = bf16[520,512]{1,0:T(8,128)(2,1)} fusion(bf16[520,512]{1,0:T(8,128)(2,1)} %collective-permute-done.18, bf16[520,512]{1,0:T(8,128)(2,1)} %collective-permute-done.16, pred[]{:T(512)S(6)} %ne.3), kind=kLoop, calls=%fused_computation | loop fusion | flops 266240 | bytes 1597441 | tf_op jit(solution)/shard_map/cond/branch_1_fun/jit(_where)/select_n | solution.py:183
  79.4 0.0 collective-permute-done.17
  79.4 3.0 %final.1 = (f32[512,512]{1,0:T(8,128)}, bf16[512,512]{1,0:T(8,128)(2,1)}, bf16[1,512]{1,0:T(2,128)(2,1)}, bf16[1,512]{1,0:T(2,128)(2,1)}) custom-call(s32[1]{0:T(128)} %get-tuple-element.184.took_ref, f32[512,512]{1,0:T(8,128)} %get-tuple-element.185.own_ref, bf16[520,512]{1,0:T(8,128)(2,1)} %get-tuple-element.186.mom_ref.mom_g_ref, ...), custom_call_target="tpu_custom_call" | custom-call | tf_op jit(solution)/shard_map/final/pallas_call | solution.py:203
Async XLA Ops:
  4.4 7.1 %copy-start.1 = (bf16[1,512]{1,0:T(2,128)(2,1)S(1)}, bf16[1,512]{1,0:T(2,128)(2,1)}, u32[]{:S(2)}) copy-start(bf16[1,512]{1,0:T(2,128)(2,1)} %get-tuple-element.111.gain_ref) | copy-start | bytes 3076 | tf_op jit(solution)/shard_map/cond
  4.4 49.3 %copy-start.7 = (bf16[1,512]{1,0:T(2,128)(2,1)S(1)}, bf16[1,512]{1,0:T(2,128)(2,1)}, u32[]{:S(2)}) copy-start(bf16[1,512]{1,0:T(2,128)(2,1)} %get-tuple-element.114.gain_moment_ref) | copy-start | bytes 3076 | tf_op jit(solution)/shard_map/cond
  4.5 46.8 %all-to-all-start.5 = ((bf16[8,192,1024]{2,1,0:T(8,128)(2,1)}), bf16[8,192,1024]{2,1,0:T(8,128)(2,1)S(1)}, u32[]{:S(2)}, u32[]{:S(2)}) async-start(bf16[8,192,1024]{2,1,0:T(8,128)(2,1)} %pack.7), calls=%async_computation.5 | async-start | bytes 6291456 | tf_op jit(solution)/shard_map/cond/branch_1_fun/all_to_all | solution.py:152
  13.6 17.0 %collective-permute-start.16 = (bf16[520,512]{1,0:T(8,128)(2,1)}, bf16[520,512]{1,0:T(8,128)(2,1)}, u32[]{:S(2)}, u32[]{:S(2)}) collective-permute-start(bf16[520,512]{1,0:T(8,128)(2,1)} %early.7), channel_id=1, source_target_pairs={{0,240},{8,248},{16,0},{24,8},{32,16},{40,24},{48,32},{56,40},{64,... | collective-permute-start | bytes 1597448 | tf_op jit(solution)/shard_map/cond/branch_1_fun/ppermute | solution.py:31
  51.2 26.2 %collective-permute-start.18 = (bf16[520,512]{1,0:T(8,128)(2,1)}, bf16[520,512]{1,0:T(8,128)(2,1)}, u32[]{:S(2)}, u32[]{:S(2)}) collective-permute-start(bf16[520,512]{1,0:T(8,128)(2,1)} %collective-permute-done.16), channel_id=1, source_target_pairs={{240,496},{248,504},{496,240},{504,248},{241,497},{249,505},{497,2... | collective-permute-start | bytes 1597448 | tf_op jit(solution)/shard_map/cond/branch_1_fun/ppermute | solution.py:39
  57.2 22.1 %collective-permute-start.17 = (bf16[520,512]{1,0:T(8,128)(2,1)}, bf16[520,512]{1,0:T(8,128)(2,1)}, u32[]{:S(2)}, u32[]{:S(2)}) collective-permute-start(bf16[520,512]{1,0:T(8,128)(2,1)} %grad.7.mom_ref), channel_id=1, source_target_pairs={{0,496},{8,504},{16,0},{24,8},{32,16},{40,24},{48,32},{56,40},{64,... | collective-permute-start | bytes 1597448 | tf_op jit(solution)/shard_map/cond/branch_1_fun/ppermute | solution.py:25
where the time goes:
time: 82.8 us; the launch traced here: 82.3 us
  waiting for transfers between devices  50.5 us (61%)
  starting transfers between devices  14.4 us (17%)
  Pallas kernels  14.1 us (17%)
  other arithmetic  1.9 us (2%)
  between operations  1.29 us (2%)
    all_to_all x1, waiting for transfers between devices, section(): lax.all_to_all(packed, 'fsdp', split_axis=0, concat_axis=0, tiled=True)  20.7 us
    ppermute x1, waiting for transfers between devices, swap_halves(): lax.ppermute(value, 'rep', pairs)  15.8 us
    ppermute x1, waiting for transfers between devices, within_halves(): return lax.ppermute(value, 'rep', pairs)  14.1 us
    all_to_all x1, starting transfers between devices, section(): lax.all_to_all(packed, 'fsdp', split_axis=0, concat_axis=0, tiled=True)  7.06 us
    pallas_call x1, Pallas kernels, section(): pl.pallas_call(grad_kernel, in_specs=[VMEM] * 5, out_specs=VMEM, out_shap...  3.48 us
    pallas_call x1, Pallas kernels, section(): pl.pallas_call(pack_kernel, grid=(tokens // block,), in_specs=[pl.BlockSp...  3.13 us
    pallas_call x1, Pallas kernels, shards(): pl.pallas_call(final_kernel, grid=(rows // block,), in_specs=[pl.BlockSpe...  2.96 us
    ppermute x1, starting transfers between devices, within_halves(): return lax.ppermute(value, 'rep', pairs)  2.91 us
  transfers between devices with their start and end apart: 4, of which 3 were waited for; matrix products, arithmetic and copies ran while one was open for 2% of the time, Pallas kernels for 10%

commit v1 on v0

--- a/solution.py
+++ b/solution.py
@@ -121,7 +121,14 @@
         name="early",
     )(master, norm_gains)
     half = lax.axis_size("rep") // 2
-    peer_early = from_peer(early, distance) if far else within_halves(early, distance)
+    if far:
+        peer_early = from_peer(early, distance)
+    elif distance == 1:
+        swapped, took = swap_halves(early, 0, distance)
+        peer_early = within_halves(jnp.where(took != 0, swapped, early), distance)
+        swapped, took = early, jnp.zeros_like(took)
+    else:
+        peer_early = within_halves(early, distance)
 
     def own_step(master, mom):
         return pl.pallas_call(
@@ -176,6 +183,8 @@
     elif far:
         (mom,) = section(ROWS, *operands)
         swapped, took = early, jnp.zeros((1,), jnp.int32)
+    elif distance == 1:
+        (mom,) = section(ROWS, *operands)
     else:
         mom, peer_early = section(ROWS, *operands, peer_early)
         swapped, took = swap_halves(peer_early, half - distance, half)

time: 82.8 us -> 122 us (1.47)
  the two profiles are of different devices: /device:TPU:480 before, /device:TPU:64 now
where the time goes in v1:
time: 122 us; the launch traced here: 121 us
  waiting for transfers between devices  74.7 us (61%)
  starting transfers between devices  30.4 us (25%)
  Pallas kernels  14.2 us (12%)
  between operations  1.29 us (1%)
    ppermute x1, waiting for transfers between devices, from_peer(): lax.ppermute(value, 'rep', [(source, (source - steps) % count) for source...  35.6 us
    all_to_all x1, waiting for transfers between devices, section(): lax.all_to_all(packed, 'fsdp', split_axis=0, concat_axis=0, tiled=True)  26.7 us
    ppermute x1, waiting for transfers between devices, within_halves(): return lax.ppermute(value, 'rep', pairs)  12.4 us
    ppermute x1, starting transfers between devices, from_peer(): lax.ppermute(value, 'rep', [(source, (source - steps) % count) for source...  11 us
    ppermute x1, starting transfers between devices, within_halves(): return lax.ppermute(value, 'rep', pairs)  10.9 us
    all_to_all x1, starting transfers between devices, section(): lax.all_to_all(packed, 'fsdp', split_axis=0, concat_axis=0, tiled=True)  7.06 us
    pallas_call x1, Pallas kernels, section(): pl.pallas_call(grad_kernel, in_specs=[VMEM] * 5, out_specs=VMEM, out_shap...  3.48 us
    pallas_call x1, Pallas kernels, section(): pl.pallas_call(pack_kernel, grid=(tokens // block,), in_specs=[pl.BlockSp...  3.18 us
  transfers between devices with their start and end apart: 4, of which 3 were waited for; matrix products, arithmetic and copies ran while one was open for 0% of the time, Pallas kernels for 7%

profile of v1, /device:TPU:64, one launch (start us, length us, event | category | flops | bytes accessed | tf_op | source)
XLA Modules:
  0.0 121.3 jit_solution(12118459872852386032)
XLA Ops:
  1.3 117.0 %conditional.3 = (f32[512,512]{1,0:T(8,128)}, bf16[520,512]{1,0:T(8,128)(2,1)}, bf16[520,512]{1,0:T(8,128)(2,1)}, bf16[520,512]{1,0:T(8,128)(2,1)}, bf16[520,512]{1,0:T(8,128)(2,1)}, /*index=5*/s32[1]{0:T(128)}) conditional(s32[]{:T(128)} %clamp.3, (f32[1,512,512]{2,1,0:T(8,128)}, bf16[1,192,4096]{2,1,0:T(8,128)(2,1)}, ...), branch_computations={%region_0.1_spmd, %region_1.2_spmd, %region_2.3_spmd, %region_3.6_... | conditional | flops 266254 | bytes 17432972 | solution.py:203
  1.3 3.2 %pack.9 = bf16[8,192,1024]{2,1,0:T(8,128)(2,1)} custom-call(bf16[192,4096]{1,0:T(8,128)(2,1)} %bitcast.66, bf16[192,512]{1,0:T(8,128)(2,1)} %bitcast.78), custom_call_target="tpu_custom_call" | custom-call | tf_op jit(solution)/shard_map/cond/branch_3_fun/pack/pallas_call | solution.py:148
  4.5 0.0 copy-start.3
  4.5 0.0 copy-start.9
  4.5 7.1 %all-to-all-start.1 = ((bf16[8,192,1024]{2,1,0:T(8,128)(2,1)}), bf16[8,192,1024]{2,1,0:T(8,128)(2,1)S(1)}, u32[]{:S(2)}, u32[]{:S(2)}) async-start(bf16[8,192,1024]{2,1,0:T(8,128)(2,1)} %pack.9), calls=%async_computation.1 | async-start | bytes 6291456 | tf_op jit(solution)/shard_map/cond/branch_3_fun/all_to_all | solution.py:159
  11.6 0.0 copy-done.3
  11.6 2.1 %early.9 = bf16[520,512]{1,0:T(8,128)(2,1)} custom-call(f32[512,512]{1,0:T(8,128)} %bitcast.52, bf16[1,512]{1,0:T(2,128)(2,1)S(1)} %copy-done.3), custom_call_target="tpu_custom_call" | custom-call | tf_op jit(solution)/shard_map/cond/branch_3_fun/early/pallas_call | solution.py:118
  13.6 10.9 %collective-permute-start.6 = (bf16[520,512]{1,0:T(8,128)(2,1)}, bf16[520,512]{1,0:T(8,128)(2,1)}, u32[]{:S(2)}, u32[]{:S(2)}) collective-permute-start(bf16[520,512]{1,0:T(8,128)(2,1)} %early.9), channel_id=1, source_target_pairs={{0,192},{8,200},{16,208},{24,216},{32,224},{40,232},{48,240},{56,2... | collective-permute-start | bytes 1597448 | tf_op jit(solution)/shard_map/cond/branch_3_fun/ppermute | solution.py:31
  24.6 26.7 %all-to-all-done.1 = bf16[8,192,1024]{2,1,0:T(8,128)(2,1)S(1)} async-done(((bf16[8,192,1024]{2,1,0:T(8,128)(2,1)}), bf16[8,192,1024]{2,1,0:T(8,128)(2,1)S(1)}, u32[]{:S(2)}, u32[]{:S(2)}) %all-to-all-start.1) | async-done | bytes 3145760 | tf_op jit(solution)/shard_map/cond/branch_3_fun/all_to_all | solution.py:159
  51.3 0.0 copy-done.9
  51.3 3.5 %grad.9 = bf16[520,512]{1,0:T(8,128)(2,1)} custom-call(bf16[1536,1024]{1,0:T(8,128)(2,1)S(1)} %bitcast.40, f32[512,512]{1,0:T(8,128)} %bitcast.53, bf16[512,512]{1,0:T(8,128)(2,1)} %bitcast.72, bf16[1,512]{1,0:T(2,128)(2,1)S(1)} %copy-done.3, bf16[1,512]{1,0:T(2,128)(2,1)S(1)} %copy-done.9), custom_call_target="tpu_custom_call" | custom-call | tf_op jit(solution)/shard_map/cond/branch_3_fun/grad/pallas_call | solution.py:165
  54.8 11.0 %collective-permute-start.5 = (bf16[520,512]{1,0:T(8,128)(2,1)}, bf16[520,512]{1,0:T(8,128)(2,1)}, u32[]{:S(2)}, u32[]{:S(2)}) collective-permute-start(bf16[520,512]{1,0:T(8,128)(2,1)} %grad.9), channel_id=1, source_target_pairs={{0,448},{8,456},{16,464},{24,472},{32,480},{40,488},{48,496},{56,5... | collective-permute-start | bytes 1597448 | tf_op jit(solution)/shard_map/cond/branch_3_fun/ppermute | solution.py:25
  66.4 12.4 %collective-permute-done.6 = bf16[520,512]{1,0:T(8,128)(2,1)} collective-permute-done((bf16[520,512]{1,0:T(8,128)(2,1)}, bf16[520,512]{1,0:T(8,128)(2,1)}, u32[]{:S(2)}, u32[]{:S(2)}) %collective-permute-start.6) | collective-permute-done | bytes 532512 | tf_op jit(solution)/shard_map/cond/branch_3_fun/ppermute | solution.py:31
  78.7 3.9 %conditional.4 = (f32[512,512]{1,0:T(8,128)}, bf16[520,512]{1,0:T(8,128)(2,1)}, s32[1]{0:T(128)}) conditional(s32[]{:T(128)} %convert_element_type.12, (f32[512,512]{1,0:T(8,128)}, bf16[520,512]{1,0:T(8,128)(2,1)}, bf16[520,512]{1,0:T(8,128)(2,1)}) %tuple.78, (bf16[520,512]{1,0:T(8,128)(2,1)}, f32[512,512]{1,0:T(8,128)}, ...), branch_computations={%region_4.4_spmd, %region_5.5_spmd} | conditional | flops 13 | bytes 2130105
  78.7 1.5 %collective-permute-start.4 = (bf16[520,512]{1,0:T(8,128)(2,1)}, bf16[520,512]{1,0:T(8,128)(2,1)}, u32[]{:S(2)}, u32[]{:S(2)}) collective-permute-start(bf16[520,512]{1,0:T(8,128)(2,1)} %get-tuple-element.129), channel_id=1, source_target_pairs={{192,448},{200,456},{208,464},{216,472},{224,480},{232,488},{240,4... | collective-permute-start | bytes 1597448 | tf_op jit(solution)/shard_map/cond/branch_3_fun/cond/branch_1_fun/ppermute | solution.py:39
  80.2 2.5 %own.12 = f32[512,512]{1,0:T(8,128)} custom-call(f32[512,512]{1,0:T(8,128)} %get-tuple-element.127.master_ref, bf16[520,512]{1,0:T(8,128)(2,1)} %get-tuple-element.128.mom_ref), custom_call_target="tpu_custom_call" | custom-call | tf_op jit(solution)/shard_map/cond/branch_3_fun/cond/branch_1_fun/own/pallas_call | solution.py:134
  82.7 0.0 collective-permute-done.4
  82.7 35.6 %collective-permute-done.5 = bf16[520,512]{1,0:T(8,128)(2,1)} collective-permute-done((bf16[520,512]{1,0:T(8,128)(2,1)}, bf16[520,512]{1,0:T(8,128)(2,1)}, u32[]{:S(2)}, u32[]{:S(2)}) %collective-permute-start.5) | collective-permute-done | bytes 532512 | tf_op jit(solution)/shard_map/cond/branch_3_fun/ppermute | solution.py:25
  118.3 3.0 %final.1 = (f32[512,512]{1,0:T(8,128)}, bf16[512,512]{1,0:T(8,128)(2,1)}, bf16[1,512]{1,0:T(2,128)(2,1)}, bf16[1,512]{1,0:T(2,128)(2,1)}) custom-call(s32[1]{0:T(128)} %get-tuple-element.182.took_ref, f32[512,512]{1,0:T(8,128)} %get-tuple-element.183.own_ref, bf16[520,512]{1,0:T(8,128)(2,1)} %get-tuple-element.184.mom_ref.mom_g_ref, ...), custom_call_target="tpu_custom_call" | custom-call | tf_op jit(solution)/shard_map/final/pallas_call | solution.py:212
Async XLA Ops:
  4.5 7.1 %copy-start.3 = (bf16[1,512]{1,0:T(2,128)(2,1)S(1)}, bf16[1,512]{1,0:T(2,128)(2,1)}, u32[]{:S(2)}) copy-start(bf16[1,512]{1,0:T(2,128)(2,1)} %get-tuple-element.134.gain_ref) | copy-start | bytes 3076 | tf_op jit(solution)/shard_map/cond
  4.5 46.8 %copy-start.9 = (bf16[1,512]{1,0:T(2,128)(2,1)S(1)}, bf16[1,512]{1,0:T(2,128)(2,1)}, u32[]{:S(2)}) copy-start(bf16[1,512]{1,0:T(2,128)(2,1)} %get-tuple-element.135.gain_moment_ref) | copy-start | bytes 3076 | tf_op jit(solution)/shard_map/cond
  4.5 46.8 %all-to-all-start.1 = ((bf16[8,192,1024]{2,1,0:T(8,128)(2,1)}), bf16[8,192,1024]{2,1,0:T(8,128)(2,1)S(1)}, u32[]{:S(2)}, u32[]{:S(2)}) async-start(bf16[8,192,1024]{2,1,0:T(8,128)(2,1)} %pack.9), calls=%async_computation.1 | async-start | bytes 6291456 | tf_op jit(solution)/shard_map/cond/branch_3_fun/all_to_all | solution.py:159
  13.6 65.1 %collective-permute-start.6 = (bf16[520,512]{1,0:T(8,128)(2,1)}, bf16[520,512]{1,0:T(8,128)(2,1)}, u32[]{:S(2)}, u32[]{:S(2)}) collective-permute-start(bf16[520,512]{1,0:T(8,128)(2,1)} %early.9), channel_id=1, source_target_pairs={{0,192},{8,200},{16,208},{24,216},{32,224},{40,232},{48,240},{56,2... | collective-permute-start | bytes 1597448 | tf_op jit(solution)/shard_map/cond/branch_3_fun/ppermute | solution.py:31
  54.8 63.6 %collective-permute-start.5 = (bf16[520,512]{1,0:T(8,128)(2,1)}, bf16[520,512]{1,0:T(8,128)(2,1)}, u32[]{:S(2)}, u32[]{:S(2)}) collective-permute-start(bf16[520,512]{1,0:T(8,128)(2,1)} %grad.9), channel_id=1, source_target_pairs={{0,448},{8,456},{16,464},{24,472},{32,480},{40,488},{48,496},{56,5... | collective-permute-start | bytes 1597448 | tf_op jit(solution)/shard_map/cond/branch_3_fun/ppermute | solution.py:25
  78.7 3.9 %collective-permute-start.4 = (bf16[520,512]{1,0:T(8,128)(2,1)}, bf16[520,512]{1,0:T(8,128)(2,1)}, u32[]{:S(2)}, u32[]{:S(2)}) collective-permute-start(bf16[520,512]{1,0:T(8,128)(2,1)} %get-tuple-element.129), channel_id=1, source_target_pairs={{192,448},{200,456},{208,464},{216,472},{224,480},{232,488},{240,4... | collective-permute-start | bytes 1597448 | tf_op jit(solution)/shard_map/cond/branch_3_fun/cond/branch_1_fun/ppermute | solution.py:39

commit v2 on v1

--- a/solution.py
+++ b/solution.py
@@ -114,7 +114,7 @@
     rows, kv = master.shape
     parts = lax.axis_size("fsdp")
     far = distance * 2 == lax.axis_size("rep")
-    far_along = 8 <= distance and not far
+    swaps_inside = (8 <= distance or distance == 2) and not far
     early = pl.pallas_call(
         early_kernel,
         out_shape=jax.ShapeDtypeStruct((rows + EXTRA, kv), bf16),
@@ -123,8 +123,8 @@
     half = lax.axis_size("rep") // 2
     if far:
         peer_early = from_peer(early, distance)
-    elif distance == 1:
-        swapped, took = swap_halves(early, 0, distance)
+    elif distance <= 2:
+        swapped, took = swap_halves(early, 0, 1)
         peer_early = within_halves(jnp.where(took != 0, swapped, early), distance)
         swapped, took = early, jnp.zeros_like(took)
     else:
@@ -140,7 +140,8 @@
     def between(first, master, mom, peer_early):
         if first:
             peer_early, master = lax.optimization_barrier((peer_early, master))
-        swapped, took = swap_halves(peer_early, half - distance, half)
+        low = half - distance if distance > 2 else half - distance + 1
+        swapped, took = swap_halves(peer_early, low, half)
         return own_step(master, mom), swapped, took
 
     def section(block, *operands):
@@ -172,7 +173,7 @@
         return (mom, *early)
 
     operands = (inputs, upstream, master, moment, norm_gains, gain_moments)
-    if far_along:
+    if swaps_inside:
         (mom,) = section(ROWS, *operands)
         peer_mom = from_peer(mom, distance)
         sure = step_count >= 0
@@ -188,9 +189,7 @@
     else:
         mom, peer_early = section(ROWS, *operands, peer_early)
         swapped, took = swap_halves(peer_early, half - distance, half)
-        if distance == 2:
-            peer_early, took = jnp.where(took != 0, swapped, peer_early), jnp.zeros_like(took)
-    if not far_along:
+    if not swaps_inside:
         peer_mom = from_peer(mom, distance)
         own = own_step(master, mom)
     return own, mom, peer_mom, peer_early, swapped, took

time: 122 us -> 80.8 us (0.66)
  the two profiles are of different devices: /device:TPU:64 before, /device:TPU:481 now
where the time goes in v2:
time: 80.8 us; the launch traced here: 80.3 us
  waiting for transfers between devices  46.5 us (58%)
  starting transfers between devices  15.7 us (19%)
  Pallas kernels  14.2 us (18%)
  other arithmetic  1.9 us (2%)
  between operations  1.29 us (2%)
    all_to_all x1, waiting for transfers between devices, section(): lax.all_to_all(packed, 'fsdp', split_axis=0, concat_axis=0, tiled=True)  30.7 us
    ppermute x2, waiting for transfers between devices, swap_halves(): lax.ppermute(value, 'rep', pairs)  15.8 us
    all_to_all x1, starting transfers between devices, section(): lax.all_to_all(packed, 'fsdp', split_axis=0, concat_axis=0, tiled=True)  6.78 us
    ppermute x2, starting transfers between devices, swap_halves(): lax.ppermute(value, 'rep', pairs)  3.67 us
    pallas_call x1, Pallas kernels, section(): pl.pallas_call(grad_kernel, in_specs=[VMEM] * 5, out_specs=VMEM, out_shap...  3.47 us
    pallas_call x1, Pallas kernels, section(): pl.pallas_call(pack_kernel, grid=(tokens // block,), in_specs=[pl.BlockSp...  3.17 us
    pallas_call x1, Pallas kernels, shards(): pl.pallas_call(final_kernel, grid=(rows // block,), in_specs=[pl.BlockSpe...  2.96 us
    ppermute x1, starting transfers between devices, within_halves(): return lax.ppermute(value, 'rep', pairs)  2.63 us
  transfers between devices with their start and end apart: 5, of which 2 were waited for; matrix products, arithmetic and copies ran while one was open for 2% of the time, Pallas kernels for 10%

profile of v2, /device:TPU:481, one launch (start us, length us, event | category | flops | bytes accessed | tf_op | source)
XLA Modules:
  0.0 80.3 jit_solution(12760575154474358988)
XLA Ops:
  1.3 76.1 %conditional.4 = (f32[512,512]{1,0:T(8,128)}, bf16[520,512]{1,0:T(8,128)(2,1)}, bf16[520,512]{1,0:T(8,128)(2,1)}, bf16[520,512]{1,0:T(8,128)(2,1)}, bf16[520,512]{1,0:T(8,128)(2,1)}, /*index=5*/s32[1]{0:T(128)}) conditional(s32[]{:T(128)} %clamp.3, (f32[1,512,512]{2,1,0:T(8,128)}, bf16[1,192,4096]{2,1,0:T(8,128)(2,1)}, ...), branch_computations={%region_0.1_spmd, %region_1.4_spmd, %region_4.5_spmd, %region_5.8_... | conditional | flops 266269 | bytes 19563130 | solution.py:202
  1.3 3.2 %pack.7 = bf16[8,192,1024]{2,1,0:T(8,128)(2,1)} custom-call(bf16[192,4096]{1,0:T(8,128)(2,1)} %bitcast.67, bf16[192,512]{1,0:T(8,128)(2,1)} %bitcast.79), custom_call_target="tpu_custom_call" | custom-call | tf_op jit(solution)/shard_map/cond/branch_1_fun/pack/pallas_call | solution.py:149
  4.5 0.0 copy-start.1
  4.5 6.8 %all-to-all-start.5 = ((bf16[8,192,1024]{2,1,0:T(8,128)(2,1)}), bf16[8,192,1024]{2,1,0:T(8,128)(2,1)S(1)}, u32[]{:S(2)}, u32[]{:S(2)}) async-start(bf16[8,192,1024]{2,1,0:T(8,128)(2,1)} %pack.7), calls=%async_computation.5 | async-start | bytes 6291456 | tf_op jit(solution)/shard_map/cond/branch_1_fun/all_to_all | solution.py:160
  11.3 0.0 copy-start.7
  11.3 0.0 copy-done.1
  11.3 2.1 %early.7 = bf16[520,512]{1,0:T(8,128)(2,1)} custom-call(f32[512,512]{1,0:T(8,128)} %bitcast.48, bf16[1,512]{1,0:T(2,128)(2,1)S(1)} %copy-done.1), custom_call_target="tpu_custom_call" | custom-call | tf_op jit(solution)/shard_map/cond/branch_1_fun/early/pallas_call | solution.py:118
  13.4 1.5 %collective-permute-start.19 = (bf16[520,512]{1,0:T(8,128)(2,1)}, bf16[520,512]{1,0:T(8,128)(2,1)}, u32[]{:S(2)}, u32[]{:S(2)}) collective-permute-start(bf16[520,512]{1,0:T(8,128)(2,1)} %early.7), channel_id=1, source_target_pairs={{0,256},{256,0},{1,257},{257,1},{2,258},{258,2},{3,259},{259,3},{4... | collective-permute-start | bytes 1597448 | tf_op jit(solution)/shard_map/cond/branch_1_fun/ppermute | solution.py:39
  14.8 0.0 collective-permute-done.19
  14.8 1.9 %broadcast_select_fusion.1 = bf16[520,512]{1,0:T(8,128)(2,1)} fusion(bf16[520,512]{1,0:T(8,128)(2,1)} %collective-permute-done.19, bf16[520,512]{1,0:T(8,128)(2,1)} %early.7, pred[]{:T(512)S(6)} %ne.7), kind=kLoop, calls=%fused_computation.1 | loop fusion | flops 266240 | bytes 1597441 | tf_op jit(solution)/shard_map/cond/branch_1_fun/jit(_where)/select_n | solution.py:128
  16.7 2.6 %collective-permute-start.20 = (bf16[520,512]{1,0:T(8,128)(2,1)}, bf16[520,512]{1,0:T(8,128)(2,1)}, u32[]{:S(2)}, u32[]{:S(2)}) collective-permute-start(bf16[520,512]{1,0:T(8,128)(2,1)} %broadcast_select_fusion.1), channel_id=1, source_target_pairs={{0,240},{8,248},{16,0},{24,8},{32,16},{40,24},{48,32},{56,40},{64,... | collective-permute-start | bytes 1597448 | tf_op jit(solution)/shard_map/cond/branch_1_fun/ppermute | solution.py:31
  19.3 30.7 %all-to-all-done.5 = bf16[8,192,1024]{2,1,0:T(8,128)(2,1)S(1)} async-done(((bf16[8,192,1024]{2,1,0:T(8,128)(2,1)}), bf16[8,192,1024]{2,1,0:T(8,128)(2,1)S(1)}, u32[]{:S(2)}, u32[]{:S(2)}) %all-to-all-start.5) | async-done | bytes 3145760 | tf_op jit(solution)/shard_map/cond/branch_1_fun/all_to_all | solution.py:160
  50.0 0.0 copy-done.7
  50.0 3.5 %grad.7 = bf16[520,512]{1,0:T(8,128)(2,1)} custom-call(bf16[1536,1024]{1,0:T(8,128)(2,1)S(1)} %bitcast.40, f32[512,512]{1,0:T(8,128)} %bitcast.49, bf16[512,512]{1,0:T(8,128)(2,1)} %bitcast.73, bf16[1,512]{1,0:T(2,128)(2,1)S(1)} %copy-done.1, bf16[1,512]{1,0:T(2,128)(2,1)S(1)} %copy-done.7), custom_call_target="tpu_custom_call" | custom-call | tf_op jit(solution)/shard_map/cond/branch_1_fun/grad/pallas_call | solution.py:166
  53.5 2.6 %collective-permute-start.18 = (bf16[520,512]{1,0:T(8,128)(2,1)}, bf16[520,512]{1,0:T(8,128)(2,1)}, u32[]{:S(2)}, u32[]{:S(2)}) collective-permute-start(bf16[520,512]{1,0:T(8,128)(2,1)} %grad.7), channel_id=1, source_target_pairs={{0,496},{8,504},{16,0},{24,8},{32,16},{40,24},{48,32},{56,40},{64,... | collective-permute-start | bytes 1597448 | tf_op jit(solution)/shard_map/cond/branch_1_fun/ppermute | solution.py:25
  56.8 0.0 collective-permute-done.20
  56.8 20.6 %conditional.5 = (f32[512,512]{1,0:T(8,128)}, bf16[520,512]{1,0:T(8,128)(2,1)}, s32[1]{0:T(128)}) conditional(s32[]{:T(128)} %convert_element_type.12, (f32[512,512]{1,0:T(8,128)}, bf16[520,512]{1,0:T(8,128)(2,1)}, bf16[520,512]{1,0:T(8,128)(2,1)}) %tuple.94, (bf16[520,512]{1,0:T(8,128)(2,1)}, f32[512,512]{1,0:T(8,128)}, ...), branch_computations={%region_2.2_spmd, %region_3.3_spmd} | conditional | flops 13 | bytes 2130105
  56.8 2.2 %collective-permute-start.1 = (bf16[520,512]{1,0:T(8,128)(2,1)}, bf16[520,512]{1,0:T(8,128)(2,1)}, u32[]{:S(2)}, u32[]{:S(2)}) collective-permute-start(bf16[520,512]{1,0:T(8,128)(2,1)} %get-tuple-element.127), channel_id=1, source_target_pairs={{248,504},{504,248},{249,505},{505,249},{250,506},{506,250},{251,5... | collective-permute-start | bytes 1597448 | tf_op jit(solution)/shard_map/cond/branch_1_fun/cond/branch_1_fun/ppermute | solution.py:39
  59.0 2.5 %own.11 = f32[512,512]{1,0:T(8,128)} custom-call(f32[512,512]{1,0:T(8,128)} %get-tuple-element.125.master_ref, bf16[520,512]{1,0:T(8,128)(2,1)} %get-tuple-element.126.mom_ref), custom_call_target="tpu_custom_call" | custom-call | tf_op jit(solution)/shard_map/cond/branch_1_fun/cond/branch_1_fun/own/pallas_call | solution.py:134
  61.6 15.8 %collective-permute-done.1 = bf16[520,512]{1,0:T(8,128)(2,1)} collective-permute-done((bf16[520,512]{1,0:T(8,128)(2,1)}, bf16[520,512]{1,0:T(8,128)(2,1)}, u32[]{:S(2)}, u32[]{:S(2)}) %collective-permute-start.1) | collective-permute-done | bytes 532512 | tf_op jit(solution)/shard_map/cond/branch_1_fun/cond/branch_1_fun/ppermute | solution.py:39
  77.3 0.0 collective-permute-done.18
  77.3 3.0 %final.1 = (f32[512,512]{1,0:T(8,128)}, bf16[512,512]{1,0:T(8,128)(2,1)}, bf16[1,512]{1,0:T(2,128)(2,1)}, bf16[1,512]{1,0:T(2,128)(2,1)}) custom-call(s32[1]{0:T(128)} %get-tuple-element.208.took_ref, f32[512,512]{1,0:T(8,128)} %get-tuple-element.209.own_ref, bf16[520,512]{1,0:T(8,128)(2,1)} %get-tuple-element.210.mom_ref.mom_g_ref, ...), custom_call_target="tpu_custom_call" | custom-call | tf_op jit(solution)/shard_map/final/pallas_call | solution.py:211
Async XLA Ops:
  4.5 6.8 %copy-start.1 = (bf16[1,512]{1,0:T(2,128)(2,1)S(1)}, bf16[1,512]{1,0:T(2,128)(2,1)}, u32[]{:S(2)}) copy-start(bf16[1,512]{1,0:T(2,128)(2,1)} %get-tuple-element.132.gain_ref) | copy-start | bytes 3076 | tf_op jit(solution)/shard_map/cond
  4.5 45.5 %all-to-all-start.5 = ((bf16[8,192,1024]{2,1,0:T(8,128)(2,1)}), bf16[8,192,1024]{2,1,0:T(8,128)(2,1)S(1)}, u32[]{:S(2)}, u32[]{:S(2)}) async-start(bf16[8,192,1024]{2,1,0:T(8,128)(2,1)} %pack.7), calls=%async_computation.5 | async-start | bytes 6291456 | tf_op jit(solution)/shard_map/cond/branch_1_fun/all_to_all | solution.py:160
  11.3 38.8 %copy-start.7 = (bf16[1,512]{1,0:T(2,128)(2,1)S(1)}, bf16[1,512]{1,0:T(2,128)(2,1)}, u32[]{:S(2)}) copy-start(bf16[1,512]{1,0:T(2,128)(2,1)} %get-tuple-element.133.gain_moment_ref) | copy-start | bytes 3076 | tf_op jit(solution)/shard_map/cond
  13.4 1.5 %collective-permute-start.19 = (bf16[520,512]{1,0:T(8,128)(2,1)}, bf16[520,512]{1,0:T(8,128)(2,1)}, u32[]{:S(2)}, u32[]{:S(2)}) collective-permute-start(bf16[520,512]{1,0:T(8,128)(2,1)} %early.7), channel_id=1, source_target_pairs={{0,256},{256,0},{1,257},{257,1},{2,258},{258,2},{3,259},{259,3},{4... | collective-permute-start | bytes 1597448 | tf_op jit(solution)/shard_map/cond/branch_1_fun/ppermute | solution.py:39
  16.7 40.1 %collective-permute-start.20 = (bf16[520,512]{1,0:T(8,128)(2,1)}, bf16[520,512]{1,0:T(8,128)(2,1)}, u32[]{:S(2)}, u32[]{:S(2)}) collective-permute-start(bf16[520,512]{1,0:T(8,128)(2,1)} %broadcast_select_fusion.1), channel_id=1, source_target_pairs={{0,240},{8,248},{16,0},{24,8},{32,16},{40,24},{48,32},{56,40},{64,... | collective-permute-start | bytes 1597448 | tf_op jit(solution)/shard_map/cond/branch_1_fun/ppermute | solution.py:31
  53.5 23.8 %collective-permute-start.18 = (bf16[520,512]{1,0:T(8,128)(2,1)}, bf16[520,512]{1,0:T(8,128)(2,1)}, u32[]{:S(2)}, u32[]{:S(2)}) collective-permute-start(bf16[520,512]{1,0:T(8,128)(2,1)} %grad.7), channel_id=1, source_target_pairs={{0,496},{8,504},{16,0},{24,8},{32,16},{40,24},{48,32},{56,40},{64,... | collective-permute-start | bytes 1597448 | tf_op jit(solution)/shard_map/cond/branch_1_fun/ppermute | solution.py:25
  56.8 20.5 %collective-permute-start.1 = (bf16[520,512]{1,0:T(8,128)(2,1)}, bf16[520,512]{1,0:T(8,128)(2,1)}, u32[]{:S(2)}, u32[]{:S(2)}) collective-permute-start(bf16[520,512]{1,0:T(8,128)(2,1)} %get-tuple-element.127), channel_id=1, source_target_pairs={{248,504},{504,248},{249,505},{505,249},{250,506},{506,250},{251,5... | collective-permute-start | bytes 1597448 | tf_op jit(solution)/shard_map/cond/branch_1_fun/cond/branch_1_fun/ppermute | solution.py:39
